TPU v7x, 256 devices: a whole 4x4x8 slice. The times are simulated.
256 devices in a mesh: tp: 2 (over z_lo), sp: 32 (over x, y, core), dp: 4 (over z_hi).
Axes of the slice: x: 4, y: 4, z: 8 (z_hi: 4, z_lo: 2; z = z_hi * 2 + z_lo), core: 2. Of those that a mesh axis runs over, the one named last changes fastest.
Arguments:
- queries: bfloat16 [16384, 4096], P(('dp', 'sp'), 'tp'), parts along dimension 0, may hold values from -256 to 256
- key_projection_rows: bfloat16 [16384, 512], P(('dp', 'sp'), 'tp'), parts along dimension 0, may hold values from -8 to 8
- values: bfloat16 [16384, 512], P(('dp', 'sp'), 'tp'), parts along dimension 0, may hold values from -6 to 6
- segment_ids: int32 [16384], P('dp'), parts along dimension 0, may hold values from 0 to 11, never falling along the last dimension, each value on 1 to 1024 neighbouring positions
- residual: bfloat16 [16384, 8192], P(('dp', 'tp'), 'sp'), parts along dimension 0, may hold values from -40 to 40
- out_weight: bfloat16 [4096, 8192], P('tp', 'sp'), may hold values from -0.09375 to 0.09375
- norm_gain: float32 [8192], P('sp'), may hold values from 0.1 to 1.9
- scale_exponent: int32 [8192], P('sp'), may hold values from 7 to 8
Outputs:
- hidden_out: bfloat16 [16384, 8192], P(('dp', 'tp'), 'sp'), parts along dimension 0
- quantized: bfloat16 [16384, 8192], P(('dp', 'tp'), 'sp'), parts along dimension 0
There are 4 independent parts, one for each index of `dp`. A program takes and returns all parts, laid end to end along the dimension named above; an argument that names none is the same for every part. Nothing has to cross between parts.
Inputs may be any that keep to these rules, and one draw needn't show every extreme that they name: `segment_ids`: never falls along the window; every document holds at most a quarter of the window's tokens, and one holds exactly that many.
All inputs are finite; a program needn't handle non-finite values.
Results may differ from a plain program's by a relative error of at most 0.0065.
Values may be sent and summed in bfloat16 or wider, within the bound.
No kernel may reach another device: no remote copies, remote signals or barrier semaphores. Data moves between devices by JAX's collectives and lax.ppermute only.
A program may use at most 64 MiB of HBM per device.

v0:
```python
import jax
import jax.numpy as jnp
from jax import lax
from jax.sharding import PartitionSpec as P

D = 8192
QUERY_HEAD_COUNT = 32
KEY_VALUE_HEADS = 4
HEAD_DIMENSION = 128
epsilon = 1e-05
limit_value = 448.0


def attend_item(query_block, key_block, value_block, query_pos, query_seg, segment_ids, key_pos):
    query_count = query_block.shape[0]
    block_rows = min(512, query_count)
    blocks = query_count // block_rows

    def one_block(packed):
        block_query, block_pos, block_seg = packed
        scores = lax.dot_general(
            block_query, key_block, (((1,), (1,)), ((), ())), preferred_element_type=jnp.float32
        ) * HEAD_DIMENSION ** (-0.5)
        visible = (key_pos[None, :] <= block_pos[:, None]) & (
            segment_ids[None, :] == block_seg[:, None]
        )
        scores = jnp.where(visible, scores, -1e30)
        largest = jnp.max(scores, axis=1, keepdims=True)
        weights = jnp.exp(scores - largest)
        row_total = jnp.sum(weights, axis=1, keepdims=True)
        probabilities = (weights / row_total).astype(jnp.bfloat16)
        return jnp.dot(probabilities, value_block, preferred_element_type=jnp.float32).astype(
            jnp.bfloat16
        )

    results = lax.map(
        one_block,
        (
            query_block.reshape(blocks, block_rows, HEAD_DIMENSION),
            query_pos.reshape(blocks, block_rows),
            query_seg.reshape(blocks, block_rows),
        ),
    )
    return results.reshape(query_count, HEAD_DIMENSION)


def body(
    queries,
    key_projection_rows,
    values,
    segment_ids,
    residual,
    out_weight,
    norm_gain,
    scale_exponent,
):
    sp_count = lax.axis_size("sp")
    token_rows = queries.shape[0]
    half_rows = token_rows // 2
    local_heads = queries.shape[1] // HEAD_DIMENSION
    item_count = 2 * local_heads
    per_device = item_count // sp_count
    window_token_rows = token_rows * sp_count
    query_count = window_token_rows // 2
    group_width = QUERY_HEAD_COUNT // KEY_VALUE_HEADS
    own_index = lax.axis_index("sp")
    query_items = jnp.transpose(
        queries.reshape(2, half_rows, local_heads, HEAD_DIMENSION), (0, 2, 1, 3)
    ).reshape(item_count, half_rows, HEAD_DIMENSION)
    query_recv = lax.all_to_all(query_items, "sp", split_axis=0, concat_axis=1, tiled=True)
    key_all, value_all = (
        lax.all_gather(key_projection_rows, "sp", axis=0, tiled=True),
        lax.all_gather(values, "sp", axis=0, tiled=True),
    )
    key_pos = jnp.arange(window_token_rows, dtype=jnp.int32)
    row_number = jnp.arange(query_count, dtype=jnp.int32)
    source_device = row_number // half_rows
    within = row_number % half_rows
    segment_grid = segment_ids.reshape(sp_count, 2, half_rows)
    number = 0
    item_index = own_index * per_device + number
    which_half = item_index // local_heads
    query_pos = source_device * token_rows + which_half * half_rows + within
    query_seg = lax.dynamic_index_in_dim(segment_grid, which_half, 1, keepdims=False).reshape(
        query_count
    )
    shared_rows = item_index % local_heads // group_width
    key_block = lax.dynamic_slice_in_dim(key_all, shared_rows * HEAD_DIMENSION, HEAD_DIMENSION, 1)
    value_block = lax.dynamic_slice_in_dim(
        value_all, shared_rows * HEAD_DIMENSION, HEAD_DIMENSION, 1
    )
    outputs = [
        attend_item(
            query_recv[number], key_block, value_block, query_pos, query_seg, segment_ids, key_pos
        )
    ]
    own_outputs = jnp.stack(outputs)
    column_count = out_weight.shape[1]
    start_sum = jnp.zeros((sp_count, 2, half_rows, column_count), jnp.float32)
    pieces = lax.all_gather(own_outputs, "sp", axis=0, tiled=True)

    def add_one(number, current):
        head_number = number % local_heads
        which_half = number // local_heads
        head_weight = lax.dynamic_slice_in_dim(
            out_weight, head_number * HEAD_DIMENSION, HEAD_DIMENSION, 0
        )
        chosen = lax.dynamic_index_in_dim(pieces, number, 0, keepdims=False)
        product_term = jnp.dot(chosen, head_weight, preferred_element_type=jnp.float32).reshape(
            sp_count, 1, half_rows, column_count
        )
        corner = (0, which_half, 0, 0)
        earlier = lax.dynamic_slice(current, corner, (sp_count, 1, half_rows, column_count))
        return lax.dynamic_update_slice(current, earlier + product_term, corner)

    combined = lax.fori_loop(0, pieces.shape[0], add_one, start_sum)
    flattened = combined.reshape(window_token_rows, column_count)
    share_rows = window_token_rows // lax.axis_size("tp")
    whole_sum = lax.psum(flattened, "tp")
    summed = lax.dynamic_slice_in_dim(whole_sum, lax.axis_index("tp") * share_rows, share_rows, 0)
    projected = summed.astype(jnp.bfloat16)
    hidden_out = (residual.astype(jnp.float32) + projected.astype(jnp.float32)).astype(jnp.bfloat16)
    widened = hidden_out.astype(jnp.float32)
    square_sum = lax.psum(jnp.sum(widened * widened, axis=1), "sp")
    mean_square = (square_sum / D)[:, None]
    normed = widened * lax.rsqrt(mean_square + epsilon) * norm_gain[None, :]
    clip_bound = (limit_value * jnp.exp2(-scale_exponent.astype(jnp.float32)))[None, :]
    quantized = jnp.clip(normed, -clip_bound, clip_bound).astype(jnp.bfloat16)
    return (hidden_out, quantized)


def solution(mesh):
    in_specs = (
        P(("dp", "sp"), "tp"),
        P(("dp", "sp"), "tp"),
        P(("dp", "sp"), "tp"),
        P("dp"),
        P(("dp", "tp"), "sp"),
        P("tp", "sp"),
        P("sp"),
        P("sp"),
    )
    out_specs = (P(("dp", "tp"), "sp"), P(("dp", "tp"), "sp"))
    return jax.shard_map(body, mesh=mesh, in_specs=in_specs, out_specs=out_specs, check_vma=False)
```

profile of v0, /device:TPU:1, one launch (start us, length us, event | category | flops | bytes accessed | tf_op | source)
XLA Modules:
  0.0 569.2 jit_solution(7606608849317972235)
XLA Ops:
  10.8 8.6 %all-to-all-start = ((bf16[32,64,128]{2,1,0:T(8,128)(2,1)}), bf16[32,64,128]{2,1,0:T(8,128)(2,1)S(1)}, u32[]{:S(2)}, u32[]{:S(2)}) async-start(bf16[32,64,128]{2,1,0:T(8,128)(2,1)} %bitcast.4), calls=%async_computation | async-start | bytes 1048576 | tf_op jit(solution)/shard_map/all_to_all | solution.py:70
  19.8 43.6 %all-gather.6.cloned.1.call-done = bf16[4096,256]{1,0:T(8,128)(2,1)} async-done(((bf16[128,256]{1,0:T(8,128)(2,1)}), bf16[4096,256]{1,0:T(8,128)(2,1)}) %all-gather.6.cloned.1.call-update) | async-done | bytes 2097168 | tf_op jit(solution)/shard_map/all_gather | solution.py:73
  64.6 49.3 %all-gather.4.cloned.1.call-done = bf16[4096,256]{1,0:T(8,128)(2,1)} async-done(((bf16[128,256]{1,0:T(8,128)(2,1)}), bf16[4096,256]{1,0:T(8,128)(2,1)}) %all-gather.4.cloned.1.call-update) | async-done | bytes 2097168 | tf_op jit(solution)/shard_map/all_gather | solution.py:72
  115.2 24.3 %while.27 = (s32[]{:T(128)}, bf16[4,512,128]{2,1,0:T(8,128)(2,1)S(1)}, s32[4,512]{1,0:T(4,128)S(1)}, s32[4096]{0:T(1024)S(1)}, s32[4,512]{1,0:T(4,128)S(1)}, /*i...) while((s32[]{:T(128)}, ...), condition=%wide.region_3.4_spmd.clone, body=%wide.region_0.3_spmd.clone.sunk | while | flops 1096875008 | bytes 27564136 | solution.py:36
  140.3 77.1 %all-gather.8.cloned.1.call-done = bf16[32,2048,128]{2,1,0:T(8,128)(2,1)} async-done(((bf16[1,2048,128]{2,1,0:T(8,128)(2,1)}), bf16[32,2048,128]{2,1,0:T(8,128)(2,1)}) %all-gather.8.cloned.1.call-update) | async-done | bytes 16777232 | tf_op jit(solution)/shard_map/all_gather | solution.py:100
  219.9 174.8 %while.26 = (s32[]{:T(128)}, f32[32,2,64,256]{3,2,1,0:T(8,128)}, bf16[32,2048,128]{2,1,0:T(8,128)(2,1)}, bf16[2048,256]{1,0:T(8,128)(2,1)}, s32[]{:T(128)}, /*in...) while((s32[]{:T(128)}, f32[32,2,64,256]{3,2,1,0:T(8,128)}, ...), condition=%wide.region_5.6_spmd, body=%wide.region_4.5_spmd.sunk | while | flops 134742032 | bytes 10027344 | solution.py:116
  309.6 2.6 bitcast_dynamic-update-slice_fusion.2
  315.1 2.6 bitcast_dynamic-update-slice_fusion.2
  320.6 2.6 bitcast_dynamic-update-slice_fusion.2
  326.0 2.6 bitcast_dynamic-update-slice_fusion.2
  331.5 2.6 bitcast_dynamic-update-slice_fusion.2
  337.0 2.6 bitcast_dynamic-update-slice_fusion.2
  342.5 2.6 bitcast_dynamic-update-slice_fusion.2
  348.0 2.6 bitcast_dynamic-update-slice_fusion.2
  353.5 2.6 bitcast_dynamic-update-slice_fusion.2
  359.0 2.6 bitcast_dynamic-update-slice_fusion.2
  364.5 2.6 bitcast_dynamic-update-slice_fusion.2
  370.0 2.6 bitcast_dynamic-update-slice_fusion.2
  375.5 2.6 bitcast_dynamic-update-slice_fusion.2
  381.0 2.6 bitcast_dynamic-update-slice_fusion.2
  386.5 2.6 bitcast_dynamic-update-slice_fusion.2
  392.0 2.6 bitcast_dynamic-update-slice_fusion.2
  394.7 100.2 %all-reduce.1 = bf16[4096,256]{1,0:T(8,128)(2,1)S(1)} all-reduce(f32[4096,256]{1,0:T(8,128)} %bitcast.61), channel_id=1, replica_groups=mesh['tp'=2,'sp'=32,'dp'=4] {'tp'}, use_global_device_ids=true, to_apply=%region_6.7 | all-reduce | flops 1048576 | bytes 6291456 | tf_op jit(solution)/shard_map/psum | solution.py:119
  496.6 64.7 %psum.15 = f32[2048]{0:T(1024)S(1)} all-reduce(f32[2048]{0:T(1024)S(1)} %get-tuple-element.206), channel_id=1, replica_groups=mesh['tp'=2,'sp'=32,'dp'=4] {'sp'}, use_global_device_ids=true, to_apply=%region_8.9 | all-reduce | flops 2048 | bytes 16384 | tf_op jit(solution)/shard_map/psum | solution.py:124
  (128 shorter events, 168.9 us)
Async XLA Ops:
  7.2 12.3 %copy-start.2 = (s32[4096]{0:T(1024)S(1)}, s32[4096]{0:T(1024)}, u32[]{:S(2)}) copy-start(s32[4096]{0:T(1024)} %param.15) | copy-start | bytes 49156
  7.2 56.2 %all-gather.6.cloned.1.call-start = ((), (), s32[]{:S(2)}) async-start(), calls=%async_computation.2 | async-start | bytes 2162688 | tf_op jit(solution)/shard_map/all_gather | solution.py:73
  7.9 106.0 %all-gather.4.cloned.1.call-start = ((), (), s32[]{:S(2)}) async-start(), calls=%async_computation.1 | async-start | bytes 2162688 | tf_op jit(solution)/shard_map/all_gather | solution.py:72
  10.8 104.4 %all-to-all-start = ((bf16[32,64,128]{2,1,0:T(8,128)(2,1)}), bf16[32,64,128]{2,1,0:T(8,128)(2,1)S(1)}, u32[]{:S(2)}, u32[]{:S(2)}) async-start(bf16[32,64,128]{2,1,0:T(8,128)(2,1)} %bitcast.4), calls=%async_computation | async-start | bytes 1048576 | tf_op jit(solution)/shard_map/all_to_all | solution.py:70
  19.4 198.0 %all-gather.8.cloned.1.call-start = ((), (), s32[]{:S(2)}) async-start(), calls=%async_computation.3 | async-start | bytes 17301504 | tf_op jit(solution)/shard_map/all_gather | solution.py:100
  115.2 25.1 %copy-start.4 = (s32[256]{0:T(256)S(1)}, s32[256]{0:T(256)}, u32[]{:S(2)}) copy-start(s32[256]{0:T(256)} %param.19) | copy-start | bytes 3076
  139.5 0.8 copy-start.1
  394.7 166.6 %copy-start.3 = (f32[256]{0:T(256)S(1)}, f32[256]{0:T(256)}, u32[]{:S(2)}) copy-start(f32[256]{0:T(256)} %param.18) | copy-start | bytes 3076
  496.5 66.2 %copy-start = (bf16[2048,256]{1,0:T(8,128)(2,1)}, bf16[2048,256]{1,0:T(8,128)(2,1)S(1)}, u32[]{:S(2)}) copy-start(bf16[2048,256]{1,0:T(8,128)(2,1)S(1)} %get-tuple-element.207) | copy-start | bytes 3145732
Sparse Core Ops, SparseCore 0:
  10.5 52.7 all-gather.5
  65.9 47.9 all-gather.3
  140.4 76.9 all-gather.7
where the time goes:
time: 574 us; the launch traced here: 569 us
  waiting for transfers between devices  171 us (30%)
  blocking collectives  165 us (29%)
  matrix products  103 us (18%)
  local copies, waits for them, and re-layouts  98.9 us (17%)
  between operations  14 us (2%)
  starting transfers between devices  8.69 us (2%)
  other arithmetic  8.28 us (1%)
    psum x1, blocking collectives, body(): whole_sum = lax.psum(flattened, 'tp')  100 us
    dot_general x32, matrix products, add_one(): jnp.dot(chosen, head_weight, preferred_element_type=jnp.float32)  83.6 us
    all_gather x1, waiting for transfers between devices, body(): pieces = lax.all_gather(own_outputs, 'sp', axis=0, tiled=True)  77.1 us
    psum x1, blocking collectives, body(): square_sum = lax.psum(jnp.sum(widened * widened, axis=1), 'sp')  64.7 us
    dynamic_slice x32, local copies, waits for them, and re-layouts, add_one(): lax.dynamic_slice(current, corner, (sp_count, 1, half_rows, column_count))  56.2 us
    all_gather x1, waiting for transfers between devices, body(): lax.all_gather(key_projection_rows, 'sp', axis=0, tiled=True)  49.3 us
    all_gather x1, waiting for transfers between devices, body(): lax.all_gather(values, 'sp', axis=0, tiled=True)  43.6 us
    dynamic_slice x32, local copies, waits for them, and re-layouts, add_one(): chosen = lax.dynamic_index_in_dim(pieces, number, 0, keepdims=False)  34.6 us
  transfers between devices with their start and end apart: 4, of which 3 were waited for; matrix products, arithmetic and copies ran while one was open for 1% of the time, Pallas kernels for 0%

commit v1 on v0

--- a/solution.py
+++ b/solution.py
@@ -1,3 +1,4 @@
+import functools
 import jax
 import jax.numpy as jnp
 from jax import lax
@@ -9,6 +10,21 @@
 HEAD_DIMENSION = 128
 epsilon = 1e-05
 limit_value = 448.0
+
+
+def wait_windows(arr_in, axis_key, dim_at):
+    return jnp.concatenate(
+        lax.all_to_all(
+            jnp.stack(lax.axis_size(axis_key) * [arr_in], axis=0),
+            concat_axis=0,
+            axis_name=axis_key,
+            split_axis=0,
+        ),
+        axis=dim_at,
+    )
+
+
+proceed_rounds = functools.partial(wait_windows, axis_key="sp", dim_at=0)
 
 
 def attend_item(query_block, key_block, value_block, query_pos, query_seg, segment_ids, key_pos):
@@ -97,7 +113,7 @@
     own_outputs = jnp.stack(outputs)
     column_count = out_weight.shape[1]
     start_sum = jnp.zeros((sp_count, 2, half_rows, column_count), jnp.float32)
-    pieces = lax.all_gather(own_outputs, "sp", axis=0, tiled=True)
+    pieces = proceed_rounds(own_outputs)
 
     def add_one(number, current):
         head_number = number % local_heads

time: 574 us -> 772 us (1.34)
  waiting for transfers between devices: 171 us -> 326 us
  blocking collectives: 165 us -> 196 us
    all_to_all x0 -> x1, waiting for transfers between devices: none -> 232 us  [wait_windows(): lax.all_to_all(jnp.stack(lax.axis_size(axis_key) * [arr_in], axis=0), con...]
    all_gather x1 -> x0, waiting for transfers between devices: 77.1 us -> none  [body(): pieces = lax.all_gather(own_outputs, 'sp', axis=0, tiled=True)]
    psum x1, blocking collectives: 64.7 us -> 106 us  [body(): square_sum = lax.psum(jnp.sum(widened * widened, axis=1), 'sp')]
    psum x1, blocking collectives: 100 us -> 89.9 us  [body(): whole_sum = lax.psum(flattened, 'tp')]
where the time goes in v1:
time: 772 us; the launch traced here: 767 us
  waiting for transfers between devices  326 us (42%)
  blocking collectives  196 us (25%)
  local copies, waits for them, and re-layouts  104 us (13%)
  matrix products  104 us (13%)
  between operations  14.3 us (2%)
  starting transfers between devices  14.1 us (2%)
  other arithmetic  8.28 us (1%)
    all_to_all x1, waiting for transfers between devices, wait_windows(): lax.all_to_all(jnp.stack(lax.axis_size(axis_key) * [arr_in], axis=0), con...  232 us
    psum x1, blocking collectives, body(): square_sum = lax.psum(jnp.sum(widened * widened, axis=1), 'sp')  106 us
    psum x1, blocking collectives, body(): whole_sum = lax.psum(flattened, 'tp')  89.9 us
    dot_general x32, matrix products, add_one(): jnp.dot(chosen, head_weight, preferred_element_type=jnp.float32)  84.7 us
    dynamic_slice x32, local copies, waits for them, and re-layouts, add_one(): lax.dynamic_slice(current, corner, (sp_count, 1, half_rows, column_count))  56.2 us
    all_gather x1, waiting for transfers between devices, body(): lax.all_gather(key_projection_rows, 'sp', axis=0, tiled=True)  49.3 us
    all_gather x1, waiting for transfers between devices, body(): lax.all_gather(values, 'sp', axis=0, tiled=True)  43.6 us
    dynamic_slice x32, local copies, waits for them, and re-layouts, add_one(): chosen = lax.dynamic_index_in_dim(pieces, number, 0, keepdims=False)  34.6 us
  transfers between devices with their start and end apart: 4, of which 3 were waited for; matrix products, arithmetic and copies ran while one was open for 1% of the time, Pallas kernels for 0%

profile of v1, /device:TPU:1, one launch (start us, length us, event | category | flops | bytes accessed | tf_op | source)
XLA Modules:
  0.0 767.1 jit_solution(6659235724287162827)
XLA Ops:
  10.8 8.6 %all-to-all-start = ((bf16[32,64,128]{2,1,0:T(8,128)(2,1)}), bf16[32,64,128]{2,1,0:T(8,128)(2,1)S(1)}, u32[]{:S(2)}, u32[]{:S(2)}) async-start(bf16[32,64,128]{2,1,0:T(8,128)(2,1)} %bitcast.4), calls=%async_computation | async-start | bytes 1048576 | tf_op jit(solution)/shard_map/all_to_all | solution.py:86
  19.7 43.6 %all-gather.5.cloned.1.call-done = bf16[4096,256]{1,0:T(8,128)(2,1)} async-done(((bf16[128,256]{1,0:T(8,128)(2,1)}), bf16[4096,256]{1,0:T(8,128)(2,1)}) %all-gather.5.cloned.1.call-update) | async-done | bytes 2097168 | tf_op jit(solution)/shard_map/all_gather | solution.py:89
  64.6 49.3 %all-gather.3.cloned.1.call-done = bf16[4096,256]{1,0:T(8,128)(2,1)} async-done(((bf16[128,256]{1,0:T(8,128)(2,1)}), bf16[4096,256]{1,0:T(8,128)(2,1)}) %all-gather.3.cloned.1.call-update) | async-done | bytes 2097168 | tf_op jit(solution)/shard_map/all_gather | solution.py:88
  115.2 24.3 %while.27 = (s32[]{:T(128)}, bf16[4,512,128]{2,1,0:T(8,128)(2,1)S(1)}, s32[4,512]{1,0:T(4,128)S(1)}, s32[4096]{0:T(1024)S(1)}, s32[4,512]{1,0:T(4,128)S(1)}, /*i...) while((s32[]{:T(128)}, ...), condition=%wide.region_3.4_spmd.clone, body=%wide.region_0.3_spmd.clone.sunk | while | flops 1096875008 | bytes 27564136 | solution.py:52
  139.5 6.2 stack.3
  145.7 5.4 all-to-all-start.1
  151.1 231.8 %all-to-all-done.1 = bf16[32,1,2048,128]{3,2,1,0:T(8,128)(2,1)} async-done(((bf16[32,1,2048,128]{3,2,1,0:T(8,128)(2,1)}), bf16[32,1,2048,128]{3,2,1,0:T(8,128)(2,1)}, u32[]{:S(2)}, u32[]{:S(2)}) %all-to-all-start.1) | async-done | bytes 16777248 | tf_op jit(solution)/shard_map/all_to_all | solution.py:17
  385.4 176.0 %while.26 = (s32[]{:T(128)}, f32[32,2,64,256]{3,2,1,0:T(8,128)}, bf16[32,2048,128]{2,1,0:T(8,128)(2,1)}, bf16[2048,256]{1,0:T(8,128)(2,1)}, s32[]{:T(128)}, /*in...) while((s32[]{:T(128)}, f32[32,2,64,256]{3,2,1,0:T(8,128)}, ...), condition=%wide.region_5.6_spmd, body=%wide.region_4.5_spmd.sunk | while | flops 134742032 | bytes 10027344 | solution.py:132
  388.2 2.7 bitcast_dynamic-update-slice_fusion.2
  393.8 2.7 bitcast_dynamic-update-slice_fusion.2
  399.3 2.7 bitcast_dynamic-update-slice_fusion.2
  404.8 2.7 bitcast_dynamic-update-slice_fusion.2
  410.3 2.7 bitcast_dynamic-update-slice_fusion.2
  415.8 2.7 bitcast_dynamic-update-slice_fusion.2
  421.3 2.7 bitcast_dynamic-update-slice_fusion.2
  426.8 2.7 bitcast_dynamic-update-slice_fusion.2
  432.4 2.7 bitcast_dynamic-update-slice_fusion.2
  437.9 2.7 bitcast_dynamic-update-slice_fusion.2
  443.4 2.7 bitcast_dynamic-update-slice_fusion.2
  448.9 2.7 bitcast_dynamic-update-slice_fusion.2
  459.9 2.7 bitcast_dynamic-update-slice_fusion.2
  471.0 2.7 bitcast_dynamic-update-slice_fusion.2
  561.4 89.9 %all-reduce.1 = bf16[4096,256]{1,0:T(8,128)(2,1)S(1)} all-reduce(f32[4096,256]{1,0:T(8,128)} %bitcast.62), channel_id=1, replica_groups=mesh['tp'=2,'sp'=32,'dp'=4] {'tp'}, use_global_device_ids=true, to_apply=%region_6.7 | all-reduce | flops 1048576 | bytes 6291456 | tf_op jit(solution)/shard_map/psum | solution.py:135
  653.0 105.8 %psum.15 = f32[2048]{0:T(1024)S(1)} all-reduce(f32[2048]{0:T(1024)S(1)} %get-tuple-element.206), channel_id=1, replica_groups=mesh['tp'=2,'sp'=32,'dp'=4] {'sp'}, use_global_device_ids=true, to_apply=%region_8.9 | all-reduce | flops 2048 | bytes 16384 | tf_op jit(solution)/shard_map/psum | solution.py:140
  (126 shorter events, 174.2 us)
Async XLA Ops:
  7.2 12.3 %copy-start.1 = (s32[4096]{0:T(1024)S(1)}, s32[4096]{0:T(1024)}, u32[]{:S(2)}) copy-start(s32[4096]{0:T(1024)} %param.15) | copy-start | bytes 49156
  7.2 56.2 %all-gather.5.cloned.1.call-start = ((), (), s32[]{:S(2)}) async-start(), calls=%async_computation.3 | async-start | bytes 2162688 | tf_op jit(solution)/shard_map/all_gather | solution.py:89
  7.9 106.0 %all-gather.3.cloned.1.call-start = ((), (), s32[]{:S(2)}) async-start(), calls=%async_computation.2 | async-start | bytes 2162688 | tf_op jit(solution)/shard_map/all_gather | solution.py:88
  10.8 104.4 %all-to-all-start = ((bf16[32,64,128]{2,1,0:T(8,128)(2,1)}), bf16[32,64,128]{2,1,0:T(8,128)(2,1)S(1)}, u32[]{:S(2)}, u32[]{:S(2)}) async-start(bf16[32,64,128]{2,1,0:T(8,128)(2,1)} %bitcast.4), calls=%async_computation | async-start | bytes 1048576 | tf_op jit(solution)/shard_map/all_to_all | solution.py:86
  145.7 5.4 copy-start.3
  145.7 237.3 %all-to-all-start.1 = ((bf16[32,1,2048,128]{3,2,1,0:T(8,128)(2,1)}), bf16[32,1,2048,128]{3,2,1,0:T(8,128)(2,1)}, u32[]{:S(2)}, u32[]{:S(2)}) async-start(bf16[32,1,2048,128]{3,2,1,0:T(8,128)(2,1)} %stack.3), calls=%async_computation.1 | async-start | bytes 33554432 | tf_op jit(solution)/shard_map/all_to_all | solution.py:17
  561.4 197.5 %copy-start.2 = (f32[256]{0:T(256)S(1)}, f32[256]{0:T(256)}, u32[]{:S(2)}) copy-start(f32[256]{0:T(256)} %param.18) | copy-start | bytes 3076
  653.0 107.3 %copy-start = (bf16[2048,256]{1,0:T(8,128)(2,1)}, bf16[2048,256]{1,0:T(8,128)(2,1)S(1)}, u32[]{:S(2)}) copy-start(bf16[2048,256]{1,0:T(8,128)(2,1)S(1)} %get-tuple-element.207) | copy-start | bytes 3145732
Sparse Core Ops, SparseCore 0:
  10.5 52.7 all-gather.4
  65.9 47.9 all-gather.2
